TPU v7x, 512 devices: a whole 4x4x16 slice. The times are simulated.
512 devices in a mesh: adv: 8 (over y, core), imp: 64 (over z, x).
Axes of the slice: x: 4, y: 4, z: 16, core: 2. Of those that a mesh axis runs over, the one named last changes fastest.
Arguments:
- adv_embed: float32 [16384, 64], P(('adv', 'imp')), may hold values from -5 to 5
- imp_embed: float32 [32768, 64], P(('imp', 'adv')), may hold values from -5 to 5
- value_scale: float32 [16384], P('adv'), may hold values from 0.3 to 3
- spend_class: int32 [16384], P('adv'), may hold values from 0 to 7
- eligible: int32 [128, 256], P('adv', 'imp'), may hold values from 0 to 1, as said below
Outputs:
- bid_density: float32 [16384, 32768], P('adv', 'imp')
- prices: float32 [32768], P('imp')
- pacing: float32 [16384], P('adv')
Inputs may be any that keep to these rules, and one draw needn't show every extreme that they name: Every impression block is eligible for at least one advertiser block.
All inputs are finite; a program needn't handle non-finite values.
Results may differ from a plain program's by a relative error of at most 0.0002.
Values sent between devices are 32-bit elements; how exact they have to be, the bound alone decides.
A program may use at most 64 MiB of HBM per device.

v0:
```python
import jax
import jax.numpy as jnp
from jax import lax
from jax.sharding import PartitionSpec as P

BLOCK = 128
ITERS = 2


score_gain = 0.0875


def score_block(embed_rows, imp_block):
    return (
        jnp.einsum(
            "ae,ie->ai",
            embed_rows,
            imp_block,
            precision=lax.Precision.HIGHEST,
            preferred_element_type=jnp.float32,
        )
        * score_gain
    )


def per_device(adv_embed, imp_embed, value_scale, spend_class, eligible):
    imp_block = lax.all_gather(imp_embed, "adv", axis=0, tiled=True)
    scores = score_block(lax.all_gather(adv_embed, "imp", axis=0, tiled=True), imp_block)
    adv_count = scores.shape[0]
    imp_count = scores.shape[1]
    total_advs = adv_count * lax.axis_size("adv")
    total_imps = imp_count * lax.axis_size("imp")
    mask_rows = eligible.shape[0]
    mask_cols = eligible.shape[1]
    expanded = jnp.broadcast_to(
        eligible.astype(jnp.float32)[:, None, :, None], (mask_rows, BLOCK, mask_cols, BLOCK)
    )
    blocks_mask = expanded.reshape(adv_count, imp_count)
    values = value_scale[:, None] * jnp.exp(scores) * blocks_mask
    allowance = total_imps / total_advs * jnp.exp(0.3 * spend_class.astype(jnp.float32) - 1.2)
    bid_tile = blocks_mask * allowance[:, None] / total_imps
    prices = jnp.ones((imp_count,), jnp.float32)
    pacing = jnp.ones((adv_count,), jnp.float32)
    for step in range(ITERS):
        prices = lax.psum(jnp.sum(bid_tile, axis=0), "adv")
        gain = values * bid_tile / prices[None, :]
        row_totals = jnp.sum(gain, axis=1)
        spending = lax.psum(row_totals, "imp")
        pacing = allowance / jnp.maximum(spending, allowance)
        bid_tile = pacing[:, None] * gain
    return (bid_tile * total_advs, prices, pacing)


def solution(mesh):
    in_specs = (
        P(("adv", "imp"), None),
        P(("imp", "adv"), None),
        P("adv"),
        P("adv"),
        P("adv", "imp"),
    )
    out_specs = (P("adv", "imp"), P("imp"), P("adv"))
    return jax.shard_map(
        per_device, mesh=mesh, in_specs=in_specs, out_specs=out_specs, check_vma=False
    )
```

profile of v0, /device:TPU:6, one launch (start us, length us, event | category | flops | bytes accessed | tf_op | source)
XLA Modules:
  0.0 457.5 jit_solution(4606812134797121241)
XLA Ops:
  0.6 0.0 copy-start.3
  0.6 0.7 convert_element_type.7
  1.3 0.7 exponential_multiply_fusion
  2.0 1.2 multiply_reduce_fusion
  3.2 14.9 %psum.28 = f32[512]{0:T(512)S(1)} all-reduce(f32[512]{0:T(512)S(1)} %bitcast.20), channel_id=1, replica_groups=mesh['adv'=8,'imp'=64] {'adv'}, use_global_device_ids=true, to_apply=%region_1.0 | all-reduce | flops 512 | bytes 4096 | tf_op jit(solution)/shard_map/psum | solution.py:45
  18.1 13.0 %all_gather.7 = f32[512,64]{1,0:T(8,128)S(1)} all-gather(f32[64,64]{1,0:T(8,128)} %param.6), channel_id=1, replica_groups=mesh['adv'=8,'imp'=64] {'adv'}, dimensions={0}, use_global_device_ids=true | all-gather | bytes 147456 | tf_op jit(solution)/shard_map/all_gather | solution.py:27
  31.1 106.5 %all_gather.6 = f32[2048,64]{1,0:T(8,128)S(1)} all-gather(f32[32,64]{1,0:T(8,128)} %param.5), channel_id=1, replica_groups=mesh['adv'=8,'imp'=64] {'imp'}, dimensions={0}, use_global_device_ids=true | all-gather | bytes 532480 | tf_op jit(solution)/shard_map/all_gather | solution.py:28
  137.6 0.3 broadcast_in_dim.2
  138.0 0.0 copy-done.3
  138.0 0.0 copy-start
  138.0 8.0 %fusion.5 = (f32[2048]{0:T(1024)S(1)}, f32[2048,512]{0,1:T(8,128)}, f32[2048,512]{0,1:T(8,128)}) fusion(f32[512]{0:T(512)S(1)} %psum.28, f32[2048]{0:T(1024)S(1)} %get-tuple-element.8, f32[64,8,16,128]{3,2,1,0:T(8,128)S(1)} %bitcast.19, f32[2048,64]{1,0:T(8,128)S(1)} %all_gather.6, f32[512,64]{1,0:T(8,128)S(1)} %all_gather.7, f32[2048]{0:T(1024)S(1)} %copy-done.3), kind=kOutput, calls=%fused_computation.14 | convolution fusion | flops 813692928 | bytes 13264896 | tf_op jit(solution)/shard_map/ae,ie->ai/dot_general | solution.py:15
  146.0 137.2 %psum.29 = f32[2048]{0:T(1024)S(1)} all-reduce(f32[2048]{0:T(1024)S(1)} %get-tuple-element.6), channel_id=1, replica_groups=mesh['adv'=8,'imp'=64] {'imp'}, use_global_device_ids=true, to_apply=%region_3.0 | all-reduce | flops 2048 | bytes 16384 | tf_op jit(solution)/shard_map/psum | solution.py:48
  283.3 0.0 copy-done
  283.3 2.5 multiply_reduce_fusion.1
  285.8 12.4 %psum.30 = f32[512]{0:T(512)S(1)} all-reduce(f32[512]{0:T(512)S(1)} %multiply_reduce_fusion.1), channel_id=1, replica_groups=mesh['adv'=8,'imp'=64] {'adv'}, use_global_device_ids=true, to_apply=%region_5.0 | all-reduce | flops 512 | bytes 4096 | tf_op jit(solution)/shard_map/psum | solution.py:45
  298.3 0.0 copy-start.2
  298.3 4.3 fusion.4
  302.6 142.6 %psum.31 = f32[2048]{0:T(1024)S(1)} all-reduce(f32[2048]{0:T(1024)S(1)} %fusion.4), channel_id=1, replica_groups=mesh['adv'=8,'imp'=64] {'imp'}, use_global_device_ids=true, to_apply=%region_7.0 | all-reduce | flops 2048 | bytes 16384 | tf_op jit(solution)/shard_map/psum | solution.py:48
  445.2 0.0 copy-done.2
  445.2 0.0 copy-start.1
  445.3 6.9 %multiply_multiply_fusion = f32[2048,512]{0,1:T(8,128)} fusion(f32[2048]{0:T(1024)S(1)} %maximum_divide_fusion, f32[512]{0:T(512)S(1)} %psum.30, f32[2048,512]{0,1:T(8,128)} %get-tuple-element.10, f32[2048,512]{0,1:T(8,128)} %get-tuple-element.7, f32[2048]{0:T(1024)S(1)} %maximum_divide_fusion.1), kind=kLoop, calls=%fused_computation.5 | loop fusion | flops 5242880 | bytes 12601344 | tf_op jit(solution)/shard_map/mul | solution.py:51
  452.1 0.0 copy-done.1
  452.1 5.3 %copy.8 = f32[2048,512]{1,0:T(8,128)} copy(f32[2048,512]{0,1:T(8,128)} %multiply_multiply_fusion) | data formatting | bytes 8388608
  (2 shorter events, 0.0 us)
Async XLA Ops:
  0.6 137.3 %copy-start.3 = (f32[2048]{0:T(1024)S(1)}, f32[2048]{0:T(1024)}, u32[]{:S(2)}) copy-start(f32[2048]{0:T(1024)} %param.7) | copy-start | bytes 24580
  138.0 145.3 %copy-start = (s32[2048]{0:T(1024)S(1)}, s32[2048]{0:T(1024)}, u32[]{:S(2)}) copy-start(s32[2048]{0:T(1024)} %param.8) | copy-start | bytes 24580
  298.3 147.0 %copy-start.2 = (f32[512]{0:T(512)}, f32[512]{0:T(512)S(1)}, u32[]{:S(2)}) copy-start(f32[512]{0:T(512)S(1)} %psum.30) | copy-start | bytes 6148
  445.2 6.9 %copy-start.1 = (f32[2048]{0:T(1024)}, f32[2048]{0:T(1024)S(1)}, u32[]{:S(2)}) copy-start(f32[2048]{0:T(1024)S(1)} %maximum_divide_fusion) | copy-start | bytes 24580
where the time goes:
time: 462 us; the launch traced here: 457 us
  blocking collectives  427 us (92%)
  other arithmetic  16.3 us (4%)
  matrix products  8.03 us (2%)
  local copies, waits for them, and re-layouts  5.7 us (1%)
    psum x2, blocking collectives, per_device(): spending = lax.psum(row_totals, 'imp')  280 us
    all_gather x1, blocking collectives, per_device(): lax.all_gather(adv_embed, 'imp', axis=0, tiled=True)  106 us
    psum x2, blocking collectives, per_device(): prices = lax.psum(jnp.sum(bid_tile, axis=0), 'adv')  27.3 us
    all_gather x1, blocking collectives, per_device(): imp_block = lax.all_gather(imp_embed, 'adv', axis=0, tiled=True)  13 us

commit v1 on v0

v1 whole, which is shorter than its diff:
```python
import functools

import jax
import jax.numpy as jnp
from jax import lax
from jax.experimental import pallas as pl
from jax.experimental.pallas import tpu as pltpu
from jax.sharding import PartitionSpec as P

MESH = pl.DeviceIdType.MESH
BLOCK = 128
SCORE_GAIN = 0.0875
LOG2E = 1.4426950408889634
NX = 4
NZ = 16
NA = 8
F32 = jnp.float32
BF16 = jnp.bfloat16

NEAR = (1, -1, 2, -2, 3, -3, 4, -4)
FAR_NEG = (1, 2, 3, 4)
FAR_POS = (1, 2, 3)
WINDOW = (1, -1, 2, -2)
JUMP = (5, -5)
ALL_D = (0, 1, -1, 2, -2, 3, -3, 4, -4, 5, -5, 6, -6, 7, -7, 8)

_n = 0
S_Z = {}
for _d in ALL_D[1:]:
    S_Z[_d] = _n
    _n += 1
S_X = {}
for _d in ALL_D:
    for _e in (1, 2, 3):
        S_X[_d, _e] = _n
        _n += 1
S_IMP = {}
S_P1 = {}
S_P2 = {}
for _k in range(1, NA):
    S_IMP[_k] = _n
    S_P1[_k] = _n + 1
    S_P2[_k] = _n + 2
    _n += 3
S_RX = {}
S_RZ = {}
for _round in range(2):
    for _e in (1, 2, 3):
        S_RX[_round, _e] = _n
        _n += 1
    for _d in WINDOW + JUMP + (8,):
        S_RZ[_round, _d] = _n
        _n += 1
N_SEM = _n


def split_parts(rows):
    high = rows.astype(BF16).astype(F32)
    rest = rows - high
    mid = rest.astype(BF16).astype(F32)
    low = rest - mid
    return high, mid, low


def first_half(shape):
    return lax.broadcasted_iota(jnp.int32, shape, len(shape) - 1) < 64


def twice(packed):
    turned = pltpu.roll(packed, 64, axis=len(packed.shape) - 1)
    left = first_half(packed.shape)
    return jnp.where(left, packed, turned), jnp.where(left, turned, packed)


def exchange_kernel(
    adv_hbm,
    imp_hbm,
    scale_hbm,
    class_hbm,
    elig_hbm,
    a_out,
    b_out,
    aux_out,
    adv_in,
    imp_in,
    scale_ref,
    class_ref,
    elig_ref,
    adv_buf,
    imp_buf,
    a_ref,
    b_ref,
    e_ref,
    t_ref,
    p1_buf,
    p2_buf,
    r1_ref,
    c2_ref,
    sums,
    rx_buf,
    rz_buf,
    aux_ref,
    send_sem,
    recv_sem,
    in_sem,
    out_sem,
):
    adv = lax.axis_index("adv")
    imp = lax.axis_index("imp")
    z = imp // NX
    x = lax.rem(imp, NX)

    def at_z(d):
        return lax.rem(z + (d + NZ), NZ)

    def at_x(e):
        return lax.rem(x + e, NX)

    def slot(d, e):
        return at_z(d) * NX + at_x(e)

    def to_z(d):
        return (adv, at_z(d) * NX + x)

    def to_x(e):
        return (adv, z * NX + at_x(e))

    def to_adv(k):
        return (lax.rem(adv + k, NA), imp)

    started = []

    def remote(src, dst, number, device):
        return pltpu.make_async_remote_copy(
            src_ref=src,
            dst_ref=dst,
            send_sem=send_sem.at[number],
            recv_sem=recv_sem.at[number],
            device_id=device,
            device_id_type=MESH,
        )

    def send(src, dst, number, device):
        copy = remote(src, dst, number, device)
        copy.start()
        started.append(copy)

    def arrived(ref, number):
        remote(ref, ref, number, to_x(1)).wait_recv()

    barrier = pltpu.get_barrier_semaphore()
    peers = [to_z(d) for d in NEAR] + [to_x(e) for e in (1, 2, 3)] + [to_adv(k) for k in range(1, NA)]
    for device in peers:
        pl.semaphore_signal(barrier, inc=1, device_id=device, device_id_type=MESH)

    loads = [
        pltpu.make_async_copy(src, dst, in_sem.at[n])
        for n, (src, dst) in enumerate(
            (
                (adv_hbm, adv_in),
                (imp_hbm, imp_in),
                (scale_hbm, scale_ref),
                (class_hbm, class_ref),
                (elig_hbm, elig_ref),
            )
        )
    ]
    for load in loads:
        load.start()
    for load in loads:
        load.wait()

    mine = slot(0, 0)
    adv_buf[mine] = jnp.concatenate([adv_in[0:16, :], adv_in[16:32, :]], axis=1)
    imp_buf[adv] = jnp.concatenate([imp_in[0:32, :], imp_in[32:64, :]], axis=1)
    allowance = 2.0 * jnp.exp(0.3 * class_ref[...].astype(F32) - 1.2)
    mask = elig_ref[...].astype(F32)
    p1_buf[adv] = jnp.zeros((8, BLOCK), F32)
    for cb in range(4):
        p1_buf[adv, cb : cb + 1, :] = jnp.sum(allowance * mask[:, cb : cb + 1], axis=0, keepdims=True)

    pl.semaphore_wait(barrier, len(peers))

    for d in (4, -4, 3, -3, 2, -2, 1, -1):
        send(adv_buf.at[mine], adv_buf.at[mine], S_Z[-d], to_z(d))
    for k in range(1, NA):
        send(imp_buf.at[adv], imp_buf.at[adv], S_IMP[k], to_adv(k))
    for e in (2, 1, 3):
        send(adv_buf.at[mine], adv_buf.at[mine], S_X[0, e], to_x(e))
    for k in range(1, NA):
        send(p1_buf.at[adv], p1_buf.at[adv], S_P1[k], to_adv(k))

    def pass_on(d):
        here = adv_buf.at[slot(d, 0)]
        arrived(here, S_Z[d])
        if d == -4:
            for k in FAR_NEG:
                far = -4 - k
                send(here, here, S_Z[8 if far == -8 else far], to_z(k))
        if d == 4:
            for k in FAR_POS:
                send(here, here, S_Z[4 + k], to_z(-k))
        for e in (2, 1, 3):
            send(here, here, S_X[d, e], to_x(e))

    for d in NEAR:
        pass_on(d)

    for k in range(1, NA):
        arrived(p1_buf.at[lax.rem(adv + (NA - k), NA)], S_P1[k])
    share = p1_buf[0]
    for k in range(1, NA):
        share = share + p1_buf[k]
    first_price = jnp.sum(share, axis=1, keepdims=True) / 32768.0
    weights = [mask[:, cb : cb + 1] / first_price[cb : cb + 1, :] for cb in range(4)]

    for k in range(1, NA):
        arrived(imp_buf.at[lax.rem(adv + (NA - k), NA)], S_IMP[k])
    low_half, up_half = twice(imp_buf[...] * (SCORE_GAIN * LOG2E))
    doubled = jnp.concatenate([low_half, up_half], axis=1).reshape(512, BLOCK)
    high, mid, low = split_parts(doubled)
    left = first_half((512, BLOCK))
    b_ref[:, 0:128] = jnp.where(left, high, mid).astype(BF16)
    b_ref[:, 128:256] = jnp.where(left, high, low).astype(BF16)
    b_ref[:, 256:384] = jnp.where(left, mid, high).astype(BF16)

    def chunk(d):
        p = lax.rem(z // 2 + (d + 8), 8)
        low_half, up_half = twice(adv_buf[pl.ds(p * 8, 8)])
        doubled = jnp.concatenate([low_half, up_half], axis=1).reshape(256, BLOCK)
        high, mid, low = split_parts(doubled)
        left = first_half((256, BLOCK))
        a_ref[p, :, 0:128] = high.astype(BF16)
        a_ref[p, :, 128:256] = jnp.where(left, mid, high).astype(BF16)
        a_ref[p, :, 256:384] = jnp.where(left, mid, low).astype(BF16)
        rows = a_ref[p]

        @pl.loop(0, 4)
        def _(cb):
            start = pl.multiple_of(cb * BLOCK, BLOCK)
            scores = lax.dot_general(
                b_ref[pl.ds(start, BLOCK), :],
                rows,
                (((1,), (1,)), ((), ())),
                preferred_element_type=F32,
            )
            values = jnp.exp2(scores)
            e_ref[p, cb] = values
            total = jnp.sum(values, axis=0, keepdims=True)
            t_ref[cb, pl.ds(p * 2, 1), :] = total[:, 0:128]
            t_ref[cb, pl.ds(p * 2 + 1, 1), :] = total[:, 128:256]

    def from_x(d):
        for e in (1, 2, 3):
            arrived(adv_buf.at[slot(d, NX - e)], S_X[d, e])

    for d in (0, 1, -1):
        from_x(d)
    chunk(0)
    for d in (2, -2, 3, -3):
        from_x(d)
    chunk(1)
    chunk(-1)
    for d in (5, -5, 6, -6, 7, -7, 8):
        pass_on(d)
    for d in (4, -4, 5, -5):
        from_x(d)
    chunk(2)
    chunk(-2)
    for d in (6, -6, 7, -7, 8):
        from_x(d)
    chunk(3)
    chunk(-3)
    chunk(4)

    keep = [
        pltpu.make_async_copy(a_ref, a_out, out_sem.at[0]),
        pltpu.make_async_copy(b_ref, b_out, out_sem.at[1]),
    ]
    for copy in keep:
        copy.start()

    def sum_over_imp(n, part):
        sums[n, 0] = part
        for e in (2, 1, 3):
            send(sums.at[n, 0], rx_buf.at[n, e - 1], S_RX[n, e], to_x(e))
        got = {0: part}
        for e in (1, 3, 2):
            arrived(rx_buf.at[n, e - 1], S_RX[n, e])
        total = part + rx_buf[n, 1] + (rx_buf[n, 0] + rx_buf[n, 2])
        sums[n, 1] = total
        index = {d: i for i, d in enumerate(WINDOW + JUMP + (8,))}

        def shift(which, d):
            send(sums.at[n, which], rz_buf.at[n, index[d]], S_RZ[n, d], to_z(-d))

        for d in (2, -2, 1, -1, 8):
            shift(1, d)
        for d in WINDOW:
            arrived(rz_buf.at[n, index[d]], S_RZ[n, d])
        window = total + ((rz_buf[n, 0] + rz_buf[n, 1]) + (rz_buf[n, 2] + rz_buf[n, 3]))
        sums[n, 2] = window
        for d in JUMP:
            shift(2, d)
        for d in JUMP + (8,):
            arrived(rz_buf.at[n, index[d]], S_RZ[n, d])
        return window + (rz_buf[n, 4] + rz_buf[n, 5]) + rz_buf[n, 6]

    scale = scale_ref[...]
    first_bid = allowance * scale / 32768.0
    part = t_ref[0] * weights[0]
    for cb in range(1, 4):
        part = part + t_ref[cb] * weights[cb]
    spending = sum_over_imp(0, part) * first_bid
    pacing = allowance / jnp.maximum(spending, allowance)
    row_bid = first_bid * pacing
    for cb in range(4):
        r1_ref[cb] = row_bid * weights[cb]

    mine_p2 = p2_buf.at[adv]
    p2_buf[adv] = jnp.ones((8, BLOCK), F32)

    @pl.loop(0, 4)
    def _(cb):
        total = jnp.zeros((BLOCK, BLOCK), F32)
        for p in range(8):
            for half in range(2):
                row = r1_ref[cb, pl.ds(2 * p + half, 1), :]
                total = total + e_ref[p, cb, :, half * 128 : half * 128 + 128] * row
        p2_buf[adv, pl.ds(cb, 1), :] = jnp.sum(total.T, axis=0, keepdims=True)

    for k in range(1, NA):
        send(mine_p2, mine_p2, S_P2[k], to_adv(k))
    for k in range(1, NA):
        arrived(p2_buf.at[lax.rem(adv + (NA - k), NA)], S_P2[k])
    price = p2_buf[0]
    for k in range(1, NA):
        price = price + p2_buf[k]
    inverse = 1.0 / price
    for cb in range(4):
        c2_ref[cb] = jnp.broadcast_to(inverse[cb : cb + 1, :], (BLOCK, BLOCK)).T

    @pl.loop(0, 8)
    def _(p):
        for half in range(2):
            total = jnp.zeros((8, BLOCK), F32)
            for cb in range(4):
                row = r1_ref[cb, pl.ds(2 * p + half, 1), :]
                value = e_ref[p, cb, :, half * 128 : half * 128 + 128]
                gain = (value * row) * c2_ref[cb] * value
                total = total + jnp.sum(gain.reshape(16, 8, BLOCK), axis=0)
            t_ref[0, pl.ds(2 * p + half, 1), :] = jnp.sum(total, axis=0, keepdims=True)

    spending = sum_over_imp(1, t_ref[0]) * scale
    pacing = allowance / jnp.maximum(spending, allowance)
    aux_ref[0:16] = row_bid
    aux_ref[16:32] = scale * pacing * 16384.0
    aux_ref[32:48] = pacing
    aux_ref[48:56] = price
    for cb in range(4):
        aux_ref[56 + 16 * cb : 72 + 16 * cb] = jnp.broadcast_to(weights[cb], (16, BLOCK))
    last = pltpu.make_async_copy(aux_ref, aux_out, out_sem.at[2])
    last.start()
    for copy in keep:
        copy.wait()
    for copy in started:
        copy.wait_send()
    last.wait()


def tile_kernel(a_ref, b_ref, aux_ref, out_ref, price_ref, pacing_ref):
    step = pl.program_id(0)
    price = aux_ref[48:52, :]
    price_ref[...] = price
    pacing_ref[...] = aux_ref[32:48, :]
    inverse = 1.0 / price
    for half in range(2):
        rb = step * 2 + half

        def column(start):
            row = aux_ref[pl.ds(start + rb, 1), :]
            return jnp.broadcast_to(row, (BLOCK, BLOCK)).T

        first = column(0)
        second = column(16)
        for cb in range(4):
            scores = lax.dot_general(
                a_ref[half * 128 : half * 128 + 128, :],
                b_ref[cb * 128 : cb * 128 + 128, :],
                (((1,), (1,)), ((), ())),
                preferred_element_type=F32,
            )
            value = jnp.exp2(scores)
            weight = aux_ref[pl.ds(56 + 16 * cb + rb, 1), :]
            bid = value * (first * weight)
            out_ref[half * 128 : half * 128 + 128, cb * 128 : cb * 128 + 128] = (
                bid * inverse[cb : cb + 1, :] * value * second
            )


def per_device(adv_embed, imp_embed, value_scale, spend_class, eligible):
    hbm = pl.BlockSpec(memory_space=pl.ANY)
    a_pack, b_pack, aux = pl.pallas_call(
        exchange_kernel,
        out_shape=(
            jax.ShapeDtypeStruct((8, 256, 384), BF16),
            jax.ShapeDtypeStruct((512, 384), BF16),
            jax.ShapeDtypeStruct((120, BLOCK), F32),
        ),
        in_specs=[hbm] * 5,
        out_specs=[hbm] * 3,
        scratch_shapes=[
            pltpu.VMEM((32, 64), F32),
            pltpu.VMEM((64, 64), F32),
            pltpu.VMEM((16, BLOCK), F32),
            pltpu.VMEM((16, BLOCK), jnp.int32),
            pltpu.VMEM((16, 4), jnp.int32),
            pltpu.VMEM((64, 16, BLOCK), F32),
            pltpu.VMEM((8, 32, BLOCK), F32),
            pltpu.VMEM((8, 256, 384), BF16),
            pltpu.VMEM((512, 384), BF16),
            pltpu.VMEM((8, 4, BLOCK, 256), F32),
            pltpu.VMEM((4, 16, BLOCK), F32),
            pltpu.VMEM((NA, 8, BLOCK), F32),
            pltpu.VMEM((NA, 8, BLOCK), F32),
            pltpu.VMEM((4, 16, BLOCK), F32),
            pltpu.VMEM((4, BLOCK, BLOCK), F32),
            pltpu.VMEM((2, 3, 16, BLOCK), F32),
            pltpu.VMEM((2, 3, 16, BLOCK), F32),
            pltpu.VMEM((2, 7, 16, BLOCK), F32),
            pltpu.VMEM((120, BLOCK), F32),
            pltpu.SemaphoreType.DMA((N_SEM,)),
            pltpu.SemaphoreType.DMA((N_SEM,)),
            pltpu.SemaphoreType.DMA((5,)),
            pltpu.SemaphoreType.DMA((3,)),
        ],
        compiler_params=pltpu.CompilerParams(
            collective_id=0, has_side_effects=True, vmem_limit_bytes=32 * 1024 * 1024
        ),
        name="exchange",
    )(
        adv_embed,
        imp_embed,
        value_scale.reshape(16, BLOCK),
        spend_class.reshape(16, BLOCK),
        eligible,
    )
    density, prices, pacing = pl.pallas_call(
        tile_kernel,
        grid=(8,),
        out_shape=(
            jax.ShapeDtypeStruct((2048, 512), F32),
            jax.ShapeDtypeStruct((4, BLOCK), F32),
            jax.ShapeDtypeStruct((16, BLOCK), F32),
        ),
        in_specs=[
            pl.BlockSpec((256, 384), lambda i: (i, 0)),
            pl.BlockSpec((512, 384), lambda i: (0, 0)),
            pl.BlockSpec((120, BLOCK), lambda i: (0, 0)),
        ],
        out_specs=[
            pl.BlockSpec((256, 512), lambda i: (i, 0)),
            pl.BlockSpec((4, BLOCK), lambda i: (0, 0)),
            pl.BlockSpec((16, BLOCK), lambda i: (0, 0)),
        ],
        name="tile",
    )(a_pack.reshape(2048, 384), b_pack, aux)
    return density, prices.reshape(512), pacing.reshape(2048)


def solution(mesh):
    in_specs = (
        P(("adv", "imp"), None),
        P(("imp", "adv"), None),
        P("adv"),
        P("adv"),
        P("adv", "imp"),
    )
    out_specs = (P("adv", "imp"), P("imp"), P("adv"))
    return jax.shard_map(
        per_device, mesh=mesh, in_specs=in_specs, out_specs=out_specs, check_vma=False
    )
```

time: 462 us -> 80.7 us (0.17)
  blocking collectives: 427 us -> 0 us
  Pallas kernels: 0 us -> 73.4 us
  other arithmetic: 16.3 us -> 0 us
  matrix products: 8.03 us -> 0 us
    psum x4 -> x0, blocking collectives: 307 us -> none  [the longest x2 280 us: per_device(): spending = lax.psum(row_totals, 'imp')]
    all_gather x2 -> x0, blocking collectives: 120 us -> none  [the longest x1 106 us: per_device(): lax.all_gather(adv_embed, 'imp', axis=0, tiled=True)]
    pallas_call x0 -> x2, Pallas kernels: none -> 73.4 us  [the longest x1 65.6 us: per_device(): pl.pallas_call(exchange_kernel, out_shape=(jax.ShapeDtypeStruct((8, 256,...]
    reduce_sum x3 -> x0, other arithmetic: 8.06 us -> none  [the longest x1 4.33 us: per_device(): row_totals = jnp.sum(gain, axis=1)]
    dot_general x1 -> x0, matrix products: 8.03 us -> none  [score_block(): jnp.einsum('ae,ie->ai', embed_rows, imp_block, precision=lax.Precision.HI...]
    mul x2 -> x0, other arithmetic: 7.56 us -> none  [the longest x1 6.86 us: per_device(): return (bid_tile * total_advs, prices, pacing)]
where the time goes in v1:
time: 80.7 us; the launch traced here: 80.2 us
  Pallas kernels  73.4 us (91%)
  local copies, waits for them, and re-layouts  6.15 us (8%)
    pallas_call x1, Pallas kernels, per_device(): pl.pallas_call(exchange_kernel, out_shape=(jax.ShapeDtypeStruct((8, 256,...  65.6 us
    pallas_call x1, Pallas kernels, per_device(): pl.pallas_call(tile_kernel, grid=(8,), out_shape=(jax.ShapeDtypeStruct((2...  7.86 us
    unnamed x15, local copies, waits for them, and re-layouts  6.15 us

profile of v1, /device:TPU:6, one launch (start us, length us, event | category | flops | bytes accessed | tf_op | source)
XLA Modules:
  0.0 80.2 jit_solution(15411739890239105096)
XLA Ops:
  0.6 0.8 copy.8.elig_hbm
  1.4 0.0 copy-start.3
  1.4 0.8 copy-done.3
  2.1 0.0 copy-start.4
  2.1 0.7 copy-done.4
  2.9 0.0 copy-start.5
  2.9 0.7 copy-done.5
  3.6 0.0 copy-start.6
  3.6 0.7 copy-done.6
  4.3 65.6 %exchange.1 = (bf16[8,256,384]{2,1,0:T(8,128)(2,1)S(1)}, bf16[512,384]{1,0:T(8,128)(2,1)S(1)}, f32[120,128]{1,0:T(8,128)S(1)}) custom-call(f32[32,64]{1,0:T(8,128)S(1)} %copy-done.4, f32[64,64]{1,0:T(8,128)S(1)} %copy-done.3, f32[16,128]{1,0:T(8,128)S(1)} %bitcast.6, s32[16,128]{1,0:T(8,128)S(1)} %bitcast.7, s32[16,4]{1,0:T(8,128)S(1)} %copy.8.elig_hbm), custom_call_target="tpu_custom_call" | custom-call | tf_op jit(solution)/shard_map/exchange/pallas_call | solution.py:403
  69.9 0.0 copy-start
  69.9 1.1 %copy-done = bf16[8,256,384]{2,1,0:T(8,128)(2,1)} copy-done((bf16[8,256,384]{2,1,0:T(8,128)(2,1)}, bf16[8,256,384]{2,1,0:T(8,128)(2,1)S(1)}, u32[]{:S(2)}) %copy-start) | copy-done | bytes 1572888
  71.0 0.0 copy-start.1
  71.0 0.7 copy-done.1
  71.8 0.0 copy-start.2
  71.8 0.6 copy-done.2
  72.4 7.9 %tile.1 = (f32[2048,512]{1,0:T(8,128)}, f32[4,128]{1,0:T(4,128)}, f32[16,128]{1,0:T(8,128)}) custom-call(bf16[2048,384]{1,0:T(8,128)(2,1)} %bitcast.5, bf16[512,384]{1,0:T(8,128)(2,1)} %copy-done.1, f32[120,128]{1,0:T(8,128)} %copy-done.2), custom_call_target="tpu_custom_call" | custom-call | tf_op jit(solution)/shard_map/tile/pallas_call | solution.py:448
Async XLA Ops:
  1.4 0.8 copy-start.3
  2.1 0.7 copy-start.4
  2.9 0.7 copy-start.5
  3.6 0.7 copy-start.6
  69.9 1.1 %copy-start = (bf16[8,256,384]{2,1,0:T(8,128)(2,1)}, bf16[8,256,384]{2,1,0:T(8,128)(2,1)S(1)}, u32[]{:S(2)}) copy-start(bf16[8,256,384]{2,1,0:T(8,128)(2,1)S(1)} %get-tuple-element.9) | copy-start | bytes 4718596
  71.0 0.8 copy-start.1
  71.8 0.6 copy-start.2

commit v2 on v1

v2 whole, which is shorter than its diff:
```python
import functools

import jax
import jax.numpy as jnp
from jax import lax
from jax.experimental import pallas as pl
from jax.experimental.pallas import tpu as pltpu
from jax.sharding import PartitionSpec as P

MESH = pl.DeviceIdType.MESH
BLOCK = 128
SCORE_GAIN = 0.0875
LOG2E = 1.4426950408889634
NX = 4
NZ = 16
NA = 8
F32 = jnp.float32
BF16 = jnp.bfloat16

NEAR = (1, -1, 2, -2, 3, -3, 4, -4)
FAR_NEG = (1, 2, 3, 4)
FAR_POS = (1, 2, 3)
WINDOW = (1, -1, 2, -2)
JUMP = (5, -5)
ALL_D = (0, 1, -1, 2, -2, 3, -3, 4, -4, 5, -5, 6, -6, 7, -7, 8)

_n = 0
S_Z = {}
for _d in ALL_D[1:]:
    S_Z[_d] = _n
    _n += 1
S_X = {}
for _d in ALL_D:
    for _e in (1, 2, 3):
        S_X[_d, _e] = _n
        _n += 1
S_IMP = {}
S_P1 = {}
S_P2 = {}
for _k in range(1, NA):
    S_IMP[_k] = _n
    S_P1[_k] = _n + 1
    S_P2[_k] = _n + 2
    _n += 3
S_RX = {}
S_RZ = {}
for _round in range(2):
    for _e in (1, 2, 3):
        S_RX[_round, _e] = _n
        _n += 1
    for _d in WINDOW + JUMP + (8,):
        S_RZ[_round, _d] = _n
        _n += 1
N_SEM = _n


def split_parts(rows):
    high = rows.astype(BF16).astype(F32)
    rest = rows - high
    mid = rest.astype(BF16).astype(F32)
    low = rest - mid
    return high, mid, low


def first_half(shape):
    return lax.broadcasted_iota(jnp.int32, shape, len(shape) - 1) < 64


def twice(packed):
    turned = pltpu.roll(packed, 64, axis=len(packed.shape) - 1)
    left = first_half(packed.shape)
    return jnp.where(left, packed, turned), jnp.where(left, turned, packed)


def exchange_kernel(
    adv_hbm,
    imp_hbm,
    scale_hbm,
    class_hbm,
    elig_hbm,
    g_ref,
    aux_ref,
    adv_in,
    imp_in,
    scale_ref,
    class_ref,
    elig_ref,
    adv_buf,
    imp_buf,
    a_ref,
    b_ref,
    e_ref,
    t_ref,
    p1_buf,
    p2_buf,
    r1_ref,
    c2_ref,
    sums,
    rx_buf,
    rz_buf,
    w_ref,
    send_sem,
    recv_sem,
    in_sem,
):
    adv = lax.axis_index("adv")
    imp = lax.axis_index("imp")
    z = imp // NX
    x = lax.rem(imp, NX)

    def at_z(d):
        return lax.rem(z + (d + NZ), NZ)

    def at_x(e):
        return lax.rem(x + e, NX)

    def slot(d, e):
        return at_z(d) * NX + at_x(e)

    def to_z(d):
        return (adv, at_z(d) * NX + x)

    def to_x(e):
        return (adv, z * NX + at_x(e))

    def to_adv(k):
        return (lax.rem(adv + k, NA), imp)

    started = []

    def remote(src, dst, number, device):
        return pltpu.make_async_remote_copy(
            src_ref=src,
            dst_ref=dst,
            send_sem=send_sem.at[number],
            recv_sem=recv_sem.at[number],
            device_id=device,
            device_id_type=MESH,
        )

    def send(src, dst, number, device):
        copy = remote(src, dst, number, device)
        copy.start()
        started.append(copy)

    def arrived(ref, number):
        remote(ref, ref, number, to_x(1)).wait_recv()

    loads = [
        pltpu.make_async_copy(src, dst, in_sem.at[n])
        for n, (src, dst) in enumerate(
            (
                (adv_hbm, adv_in),
                (imp_hbm, imp_in),
                (scale_hbm, scale_ref),
                (class_hbm, class_ref),
                (elig_hbm, elig_ref),
            )
        )
    ]
    for load in loads:
        load.start()

    barrier = pltpu.get_barrier_semaphore()
    peers = [to_z(d) for d in NEAR] + [to_x(e) for e in (1, 2, 3)] + [to_adv(k) for k in range(1, NA)]
    for device in peers:
        pl.semaphore_signal(barrier, inc=1, device_id=device, device_id_type=MESH)

    mine = slot(0, 0)
    loads[0].wait()
    adv_buf[mine] = jnp.concatenate([adv_in[0:16, :], adv_in[16:32, :]], axis=1)
    loads[1].wait()
    imp_buf[adv] = jnp.concatenate([imp_in[0:32, :], imp_in[32:64, :]], axis=1)
    for load in loads[2:]:
        load.wait()
    allowance = 2.0 * jnp.exp(0.3 * class_ref[...].astype(F32) - 1.2)
    mask = elig_ref[...].astype(F32).T
    p1_buf[adv] = jnp.zeros((8, BLOCK), F32)
    for cb in range(4):
        p1_buf[adv, cb : cb + 1, :] = jnp.sum(allowance * mask[:, cb : cb + 1], axis=0, keepdims=True)

    pl.semaphore_wait(barrier, len(peers))

    for d in (4, -4, 3, -3, 2, -2, 1, -1):
        send(adv_buf.at[mine], adv_buf.at[mine], S_Z[-d], to_z(d))
    for k in range(1, NA):
        send(imp_buf.at[adv], imp_buf.at[adv], S_IMP[k], to_adv(k))
    for e in (2, 1, 3):
        send(adv_buf.at[mine], adv_buf.at[mine], S_X[0, e], to_x(e))
    for k in range(1, NA):
        send(p1_buf.at[adv], p1_buf.at[adv], S_P1[k], to_adv(k))

    def pass_on(d):
        here = adv_buf.at[slot(d, 0)]
        arrived(here, S_Z[d])
        if d == -4:
            for k in FAR_NEG:
                far = -4 - k
                send(here, here, S_Z[8 if far == -8 else far], to_z(k))
        if d == 4:
            for k in FAR_POS:
                send(here, here, S_Z[4 + k], to_z(-k))
        for e in (2, 1, 3):
            send(here, here, S_X[d, e], to_x(e))

    for d in NEAR:
        pass_on(d)

    for k in range(1, NA):
        arrived(p1_buf.at[lax.rem(adv + (NA - k), NA)], S_P1[k])
    share = p1_buf[0]
    for k in range(1, NA):
        share = share + p1_buf[k]
    first_price = jnp.sum(share, axis=1, keepdims=True) / 32768.0
    weights = [mask[:, cb : cb + 1] / first_price[cb : cb + 1, :] for cb in range(4)]
    for cb in range(4):
        w_ref[cb] = jnp.broadcast_to(weights[cb], (16, BLOCK))

    for k in range(1, NA):
        arrived(imp_buf.at[lax.rem(adv + (NA - k), NA)], S_IMP[k])
    low_half, up_half = twice(imp_buf[...] * (SCORE_GAIN * LOG2E))
    doubled = jnp.concatenate([low_half, up_half], axis=1).reshape(512, BLOCK)
    high, mid, low = split_parts(doubled)
    left = first_half((512, BLOCK))
    b_ref[:, 0:128] = jnp.where(left, high, mid).astype(BF16)
    b_ref[:, 128:256] = jnp.where(left, high, low).astype(BF16)
    b_ref[:, 256:384] = jnp.where(left, mid, high).astype(BF16)

    for d in (5, -5, 6, -6, 7, -7, 8):
        pass_on(d)

    def chunk(p):
        low_half, up_half = twice(adv_buf[pl.ds(p * 8, 8)])
        doubled = jnp.concatenate([low_half, up_half], axis=1).reshape(256, BLOCK)
        high, mid, low = split_parts(doubled)
        left = first_half((256, BLOCK))
        rows = jnp.concatenate(
            [
                high.astype(BF16),
                jnp.where(left, mid, high).astype(BF16),
                jnp.where(left, mid, low).astype(BF16),
            ],
            axis=1,
        )
        a_ref[p] = rows
        for cb in range(4):
            scores = lax.dot_general(
                b_ref[cb * BLOCK : cb * BLOCK + BLOCK, :],
                rows,
                (((1,), (1,)), ((), ())),
                preferred_element_type=F32,
            )
            values = jnp.exp2(scores)
            e_ref[p, cb] = values
            total = jnp.sum(values, axis=0, keepdims=True)
            t_ref[cb, pl.ds(p * 2, 1), :] = total[:, 0:128]
            t_ref[cb, pl.ds(p * 2 + 1, 1), :] = total[:, 128:256]

    def from_x(d):
        for e in (1, 2, 3):
            arrived(adv_buf.at[slot(d, NX - e)], S_X[d, e])

    half_z = z // 2

    def chunks(first, count):
        @pl.loop(0, count)
        def _(n):
            far = first + n // 2
            chunk(lax.rem(half_z + jnp.where(lax.rem(n, 2) == 0, far, 8 - far), 8))

    for d in (0, 1, -1):
        from_x(d)
    chunks(0, 1)
    for d in (2, -2, 3, -3, 4, -4, 5, -5):
        from_x(d)
    chunks(1, 4)
    for d in (6, -6, 7, -7, 8):
        from_x(d)
    chunks(3, 3)

    def sum_over_imp(n, part, work):
        sums[n, 0] = part
        for e in (2, 1, 3):
            send(sums.at[n, 0], rx_buf.at[n, e - 1], S_RX[n, e], to_x(e))
        work(0, 2)
        for e in (1, 3, 2):
            arrived(rx_buf.at[n, e - 1], S_RX[n, e])
        total = part + rx_buf[n, 1] + (rx_buf[n, 0] + rx_buf[n, 2])
        sums[n, 1] = total
        index = {d: i for i, d in enumerate(WINDOW + JUMP + (8,))}

        def shift(which, d):
            send(sums.at[n, which], rz_buf.at[n, index[d]], S_RZ[n, d], to_z(-d))

        for d in (2, -2, 1, -1, 8):
            shift(1, d)
        work(2, 4)
        for d in WINDOW:
            arrived(rz_buf.at[n, index[d]], S_RZ[n, d])
        window = total + ((rz_buf[n, 0] + rz_buf[n, 1]) + (rz_buf[n, 2] + rz_buf[n, 3]))
        sums[n, 2] = window
        for d in JUMP:
            shift(2, d)
        work(4, 8)
        for d in JUMP + (8,):
            arrived(rz_buf.at[n, index[d]], S_RZ[n, d])
        return window + (rz_buf[n, 4] + rz_buf[n, 5]) + rz_buf[n, 6]

    def tile_values(start, stop):
        @pl.loop(start, stop)
        def _(p):
            scores = lax.dot_general(
                a_ref[p], b_ref[...], (((1,), (1,)), ((), ())), preferred_element_type=F32
            )
            g_ref[pl.ds(pl.multiple_of(p * 256, 256), 256), :] = jnp.exp2(scores)

    scale = scale_ref[...]
    first_bid = allowance * scale / 32768.0
    part = t_ref[0] * w_ref[0]
    for cb in range(1, 4):
        part = part + t_ref[cb] * w_ref[cb]
    spending = sum_over_imp(0, part, tile_values) * first_bid
    pacing = allowance / jnp.maximum(spending, allowance)
    row_bid = first_bid * pacing
    for cb in range(4):
        r1_ref[cb] = row_bid * w_ref[cb]
    r1_ref[4] = row_bid

    mine_p2 = p2_buf.at[adv]
    p2_buf[adv] = jnp.ones((8, BLOCK), F32)
    for cb in range(4):
        total = None
        for rb in range(16):
            row = r1_ref[cb, rb : rb + 1, :]
            half = rb % 2
            term = e_ref[rb // 2, cb, :, half * 128 : half * 128 + 128] * row
            total = term if total is None else total + term
        p2_buf[adv, cb : cb + 1, :] = jnp.sum(total.T, axis=0, keepdims=True)

    for k in range(1, NA):
        send(mine_p2, mine_p2, S_P2[k], to_adv(k))

    @pl.loop(0, 8)
    def _(p):
        for half in range(2):
            for cb in range(4):
                row = r1_ref[cb, pl.ds(2 * p + half, 1), :]
                value = e_ref[p, cb, :, half * 128 : half * 128 + 128]
                e_ref[p, cb, :, half * 128 : half * 128 + 128] = (value * row) * value

    for k in range(1, NA):
        arrived(p2_buf.at[lax.rem(adv + (NA - k), NA)], S_P2[k])
    price = p2_buf[0]
    for k in range(1, NA):
        price = price + p2_buf[k]
    inverse = 1.0 / price
    for cb in range(4):
        c2_ref[cb] = jnp.broadcast_to(inverse[cb : cb + 1, :], (BLOCK, BLOCK)).T

    @pl.loop(0, 8)
    def _(p):
        for half in range(2):
            total = jnp.zeros((8, BLOCK), F32)
            for cb in range(4):
                gain = e_ref[p, cb, :, half * 128 : half * 128 + 128] * c2_ref[cb]
                total = total + jnp.sum(gain.reshape(16, 8, BLOCK), axis=0)
            t_ref[0, pl.ds(2 * p + half, 1), :] = jnp.sum(total, axis=0, keepdims=True)

    def tile_gains(start, stop):
        @pl.loop(start, stop)
        def _(p):
            for half in range(2):
                rb = 2 * p + half
                rows = pl.ds(pl.multiple_of(p * 256 + half * 128, 128), 128)
                first = jnp.broadcast_to(r1_ref[4, pl.ds(rb, 1), :], (BLOCK, BLOCK)).T
                for cb in range(4):
                    value = g_ref[rows, cb * 128 : cb * 128 + 128]
                    bid = value * (first * w_ref[cb, pl.ds(rb, 1), :])
                    g_ref[rows, cb * 128 : cb * 128 + 128] = bid * inverse[cb : cb + 1, :] * value

    spending = sum_over_imp(1, t_ref[0], tile_gains) * scale
    pacing = allowance / jnp.maximum(spending, allowance)
    aux_ref[0:16] = scale * pacing * 16384.0
    aux_ref[16:32] = pacing
    aux_ref[32:40] = price
    for copy in started:
        copy.wait_send()


def scale_kernel(g_ref, aux_ref, out_hbm, price_hbm, pacing_hbm, out_ref, sem):
    small = [
        pltpu.make_async_copy(aux_ref.at[32:36], price_hbm, sem.at[8]),
        pltpu.make_async_copy(aux_ref.at[16:32], pacing_hbm, sem.at[9]),
    ]
    copies = []
    for p in range(8):
        for half in range(2):
            rb = 2 * p + half
            column = jnp.broadcast_to(aux_ref[rb : rb + 1, :], (BLOCK, BLOCK)).T
            rows = slice(rb * 128, rb * 128 + 128)
            for cb in range(4):
                columns = slice(cb * 128, cb * 128 + 128)
                out_ref[rows, columns] = g_ref[rows, columns] * column
        span = slice(p * 256, p * 256 + 256)
        copies.append(pltpu.make_async_copy(out_ref.at[span], out_hbm.at[span], sem.at[p]))
        copies[-1].start()
    for copy in small:
        copy.start()
    for copy in copies + small:
        copy.wait()


def per_device(adv_embed, imp_embed, value_scale, spend_class, eligible):
    hbm = pl.BlockSpec(memory_space=pltpu.HBM)
    vmem = pl.BlockSpec(memory_space=pltpu.VMEM)
    gains, aux = pl.pallas_call(
        exchange_kernel,
        out_shape=(
            jax.ShapeDtypeStruct((2048, 512), F32),
            jax.ShapeDtypeStruct((40, BLOCK), F32),
        ),
        in_specs=[hbm] * 5,
        out_specs=[vmem] * 2,
        scratch_shapes=[
            pltpu.VMEM((32, 64), F32),
            pltpu.VMEM((64, 64), F32),
            pltpu.VMEM((16, BLOCK), F32),
            pltpu.VMEM((16, BLOCK), jnp.int32),
            pltpu.VMEM((4, 16), jnp.int32),
            pltpu.VMEM((64, 16, BLOCK), F32),
            pltpu.VMEM((8, 32, BLOCK), F32),
            pltpu.VMEM((8, 256, 384), BF16),
            pltpu.VMEM((512, 384), BF16),
            pltpu.VMEM((8, 4, BLOCK, 256), F32),
            pltpu.VMEM((4, 16, BLOCK), F32),
            pltpu.VMEM((NA, 8, BLOCK), F32),
            pltpu.VMEM((NA, 8, BLOCK), F32),
            pltpu.VMEM((5, 16, BLOCK), F32),
            pltpu.VMEM((4, BLOCK, BLOCK), F32),
            pltpu.VMEM((2, 3, 16, BLOCK), F32),
            pltpu.VMEM((2, 3, 16, BLOCK), F32),
            pltpu.VMEM((2, 7, 16, BLOCK), F32),
            pltpu.VMEM((4, 16, BLOCK), F32),
            pltpu.SemaphoreType.DMA((N_SEM,)),
            pltpu.SemaphoreType.DMA((N_SEM,)),
            pltpu.SemaphoreType.DMA((5,)),
        ],
        compiler_params=pltpu.CompilerParams(
            collective_id=0, has_side_effects=True, vmem_limit_bytes=32 * 1024 * 1024
        ),
        name="exchange",
    )(
        *(
            pltpu.with_memory_space_constraint(operand, pltpu.HBM)
            for operand in (
                adv_embed,
                imp_embed,
                value_scale.reshape(16, BLOCK),
                spend_class.reshape(16, BLOCK),
                eligible.T,
            )
        )
    )
    density, prices, pacing = pl.pallas_call(
        scale_kernel,
        out_shape=(
            jax.ShapeDtypeStruct((2048, 512), F32),
            jax.ShapeDtypeStruct((4, BLOCK), F32),
            jax.ShapeDtypeStruct((16, BLOCK), F32),
        ),
        in_specs=[vmem] * 2,
        out_specs=[hbm] * 3,
        scratch_shapes=[
            pltpu.VMEM((2048, 512), F32),
            pltpu.SemaphoreType.DMA((10,)),
        ],
        compiler_params=pltpu.CompilerParams(vmem_limit_bytes=32 * 1024 * 1024),
        name="scale",
    )(gains, aux)
    return density, prices.reshape(512), pacing.reshape(2048)


def solution(mesh):
    in_specs = (
        P(("adv", "imp"), None),
        P(("imp", "adv"), None),
        P("adv"),
        P("adv"),
        P("adv", "imp"),
    )
    out_specs = (P("adv", "imp"), P("imp"), P("adv"))
    return jax.shard_map(
        per_device, mesh=mesh, in_specs=in_specs, out_specs=out_specs, check_vma=False
    )
```

time: 80.7 us -> 63.3 us (0.78)
  Pallas kernels: 73.4 us -> 61.7 us
  local copies, waits for them, and re-layouts: 6.15 us -> 0 us
    pallas_call x2, Pallas kernels: 73.4 us -> 61.7 us  [the longest x1 59.5 us: per_device(): pl.pallas_call(exchange_kernel, out_shape=(jax.ShapeDtypeStruct((2048, 51...]
    unnamed x15 -> x0, local copies, waits for them, and re-layouts: 6.15 us -> none
where the time goes in v2:
time: 63.3 us; the launch traced here: 62.4 us
  Pallas kernels  61.7 us (97%)
  between operations  0.64 us (1%)
    pallas_call x1, Pallas kernels, per_device(): pl.pallas_call(exchange_kernel, out_shape=(jax.ShapeDtypeStruct((2048, 51...  59.5 us
    pallas_call x1, Pallas kernels, per_device(): pl.pallas_call(scale_kernel, out_shape=(jax.ShapeDtypeStruct((2048, 512),...  2.2 us

profile of v2, /device:TPU:6, one launch (start us, length us, event | category | flops | bytes accessed | tf_op | source)
XLA Modules:
  0.0 62.4 jit_solution(2687331060275444630)
XLA Ops:
  0.6 59.5 %exchange.1 = (f32[2048,512]{1,0:T(8,128)S(1)}, f32[40,128]{1,0:T(8,128)S(1)}) custom-call(f32[32,64]{1,0:T(8,128)} %adv_hbm.1, f32[64,64]{1,0:T(8,128)} %imp_hbm.1, f32[16,128]{1,0:T(8,128)} %bitcast.5, s32[16,128]{1,0:T(8,128)} %bitcast.6, s32[4,16]{1,0:T(4,128)} %bitcast.7), custom_call_target="tpu_custom_call" | custom-call | tf_op jit(solution)/shard_map/exchange/pallas_call | solution.py:416
  60.2 2.2 %scale.1 = (f32[2048,512]{1,0:T(8,128)}, f32[4,128]{1,0:T(4,128)}, f32[16,128]{1,0:T(8,128)}) custom-call(f32[2048,512]{1,0:T(8,128)S(1)} %get-tuple-element.8.g_ref, f32[40,128]{1,0:T(8,128)S(1)} %get-tuple-element.9.aux_ref), custom_call_target="tpu_custom_call" | custom-call | tf_op jit(solution)/shard_map/scale/pallas_call | solution.py:464

commit v3 on v2

--- a/solution.py
+++ b/solution.py
@@ -34,23 +34,39 @@
     for _e in (1, 2, 3):
         S_X[_d, _e] = _n
         _n += 1
-S_IMP = {}
 S_P1 = {}
 S_P2 = {}
 for _k in range(1, NA):
-    S_IMP[_k] = _n
-    S_P1[_k] = _n + 1
-    S_P2[_k] = _n + 2
-    _n += 3
+    S_P1[_k] = _n
+    S_P2[_k] = _n + 1
+    _n += 2
+S_IX = {}
+S_WX = {}
+S_QX = {}
 S_RX = {}
+for _e in (1, 2, 3):
+    S_IX[_e] = _n
+    S_WX[_e] = _n + 1
+    S_QX[_e] = _n + 2
+    S_RX[_e] = _n + 3
+    _n += 4
+S_IY = {}
+S_IC = {}
+for _e in range(4):
+    for _k in range(4):
+        if _k:
+            S_IY[_e, _k] = _n
+            _n += 1
+        S_IC[_e, _k] = _n
+        _n += 1
+S_QZ = {}
+for _d in ALL_D[1:]:
+    S_QZ[_d] = _n
+    _n += 1
 S_RZ = {}
-for _round in range(2):
-    for _e in (1, 2, 3):
-        S_RX[_round, _e] = _n
-        _n += 1
-    for _d in WINDOW + JUMP + (8,):
-        S_RZ[_round, _d] = _n
-        _n += 1
+for _d in WINDOW + JUMP + (8,):
+    S_RZ[_d] = _n
+    _n += 1
 N_SEM = _n
 
 
@@ -93,6 +109,9 @@
     t_ref,
     p1_buf,
     p2_buf,
+    wl_buf,
+    quarter_buf,
+    spend_buf,
     r1_ref,
     c2_ref,
     sums,
@@ -114,8 +133,10 @@
     def at_x(e):
         return lax.rem(x + e, NX)
 
-    def slot(d, e):
-        return at_z(d) * NX + at_x(e)
+    def shard(d, e):
+        return adv_buf.at[at_z(d), at_x(e)]
+
+    partner = adv + 1 - 2 * lax.rem(adv, 2)
 
     def to_z(d):
         return (adv, at_z(d) * NX + x)
@@ -125,6 +146,9 @@
 
     def to_adv(k):
         return (lax.rem(adv + k, NA), imp)
+
+    def imps(e, whose, k):
+        return imp_buf.at[at_x(NX - e), lax.rem(whose + (NA - 2 * k), NA)]
 
     started = []
 
@@ -166,15 +190,16 @@
     for device in peers:
         pl.semaphore_signal(barrier, inc=1, device_id=device, device_id_type=MESH)
 
-    mine = slot(0, 0)
+    mine = shard(0, 0)
     loads[0].wait()
-    adv_buf[mine] = jnp.concatenate([adv_in[0:16, :], adv_in[16:32, :]], axis=1)
+    adv_buf[z, x] = jnp.concatenate([adv_in[0:16, :], adv_in[16:32, :]], axis=1)
     loads[1].wait()
-    imp_buf[adv] = jnp.concatenate([imp_in[0:32, :], imp_in[32:64, :]], axis=1)
+    imp_buf[x, adv] = jnp.concatenate([imp_in[0:32, :], imp_in[32:64, :]], axis=1)
     for load in loads[2:]:
         load.wait()
     allowance = 2.0 * jnp.exp(0.3 * class_ref[...].astype(F32) - 1.2)
-    mask = elig_ref[...].astype(F32).T
+    mask_rows = elig_ref[...].astype(F32)
+    mask = mask_rows.T
     p1_buf[adv] = jnp.zeros((8, BLOCK), F32)
     for cb in range(4):
         p1_buf[adv, cb : cb + 1, :] = jnp.sum(allowance * mask[:, cb : cb + 1], axis=0, keepdims=True)
@@ -182,16 +207,20 @@
     pl.semaphore_wait(barrier, len(peers))
 
     for d in (4, -4, 3, -3, 2, -2, 1, -1):
-        send(adv_buf.at[mine], adv_buf.at[mine], S_Z[-d], to_z(d))
-    for k in range(1, NA):
-        send(imp_buf.at[adv], imp_buf.at[adv], S_IMP[k], to_adv(k))
+        send(mine, mine, S_Z[-d], to_z(d))
+    own = imps(0, adv, 0)
     for e in (2, 1, 3):
-        send(adv_buf.at[mine], adv_buf.at[mine], S_X[0, e], to_x(e))
+        send(own, own, S_IX[e], to_x(e))
+    for k in (2, 1, 3):
+        send(own, own, S_IY[0, k], to_adv(2 * k))
+    send(own, own, S_IC[0, 0], (partner, imp))
     for k in range(1, NA):
         send(p1_buf.at[adv], p1_buf.at[adv], S_P1[k], to_adv(k))
+    for e in (2, 1, 3):
+        send(mine, mine, S_X[0, e], to_x(e))
 
     def pass_on(d):
-        here = adv_buf.at[slot(d, 0)]
+        here = shard(d, 0)
         arrived(here, S_Z[d])
         if d == -4:
             for k in FAR_NEG:
@@ -203,7 +232,15 @@
         for e in (2, 1, 3):
             send(here, here, S_X[d, e], to_x(e))
 
-    for d in NEAR:
+    for d in (1, -1, 2, -2):
+        pass_on(d)
+    for e in (1, 3, 2):
+        here = imps(e, adv, 0)
+        arrived(here, S_IX[e])
+        for k in (2, 1, 3):
+            send(here, here, S_IY[e, k], to_adv(2 * k))
+        send(here, here, S_IC[e, 0], (partner, imp))
+    for d in (3, -3, 4, -4):
         pass_on(d)
 
     for k in range(1, NA):
@@ -212,29 +249,43 @@
     for k in range(1, NA):
         share = share + p1_buf[k]
     first_price = jnp.sum(share, axis=1, keepdims=True) / 32768.0
-    weights = [mask[:, cb : cb + 1] / first_price[cb : cb + 1, :] for cb in range(4)]
+    weight_rows = mask_rows / first_price[0:4, :]
+    place = lax.broadcasted_iota(jnp.int32, (4, BLOCK), 1) // 32
+    for q in range(4):
+        spread = jnp.zeros((4, BLOCK), F32)
+        for k in range(4):
+            spread = jnp.where(place == k, weight_rows[:, 4 * q + k : 4 * q + k + 1], spread)
+        wl_buf[x, 4 * q : 4 * q + 4, :] = spread
+    for e in (2, 1, 3):
+        send(wl_buf.at[x], wl_buf.at[x], S_WX[e], to_x(e))
     for cb in range(4):
-        w_ref[cb] = jnp.broadcast_to(weights[cb], (16, BLOCK))
-
-    for k in range(1, NA):
-        arrived(imp_buf.at[lax.rem(adv + (NA - k), NA)], S_IMP[k])
-    low_half, up_half = twice(imp_buf[...] * (SCORE_GAIN * LOG2E))
-    doubled = jnp.concatenate([low_half, up_half], axis=1).reshape(512, BLOCK)
-    high, mid, low = split_parts(doubled)
-    left = first_half((512, BLOCK))
-    b_ref[:, 0:128] = jnp.where(left, high, mid).astype(BF16)
-    b_ref[:, 128:256] = jnp.where(left, high, low).astype(BF16)
-    b_ref[:, 256:384] = jnp.where(left, mid, high).astype(BF16)
-
-    for d in (5, -5, 6, -6, 7, -7, 8):
-        pass_on(d)
-
-    def chunk(p):
-        low_half, up_half = twice(adv_buf[pl.ds(p * 8, 8)])
-        doubled = jnp.concatenate([low_half, up_half], axis=1).reshape(256, BLOCK)
+        w_ref[cb] = jnp.broadcast_to(mask[:, cb : cb + 1] / first_price[cb : cb + 1, :], (16, BLOCK))
+
+    for e in (0, 1, 3, 2):
+        for k in (1, 3, 2):
+            here = imps(e, adv, k)
+            arrived(here, S_IY[e, k])
+            send(here, here, S_IC[e, k], (partner, imp))
+    for e in range(4):
+        for k in range(4):
+            arrived(imps(e, partner, k), S_IC[e, k])
+
+    @pl.loop(0, 4)
+    def _(xp):
+        low_half, up_half = twice(imp_buf[xp] * (SCORE_GAIN * LOG2E))
+        doubled = jnp.concatenate([low_half, up_half], axis=1).reshape(512, BLOCK)
         high, mid, low = split_parts(doubled)
-        left = first_half((256, BLOCK))
-        rows = jnp.concatenate(
+        left = first_half((512, BLOCK))
+        b_ref[xp, :, 0:128] = jnp.where(left, high, mid).astype(BF16)
+        b_ref[xp, :, 128:256] = jnp.where(left, high, low).astype(BF16)
+        b_ref[xp, :, 256:384] = jnp.where(left, mid, high).astype(BF16)
+
+    def operand(shards):
+        low_half, up_half = twice(shards)
+        doubled = jnp.concatenate([low_half, up_half], axis=1).reshape(shards.shape[0] * 32, BLOCK)
+        high, mid, low = split_parts(doubled)
+        left = first_half(doubled.shape)
+        return jnp.concatenate(
             [
                 high.astype(BF16),
                 jnp.where(left, mid, high).astype(BF16),
@@ -242,84 +293,77 @@
             ],
             axis=1,
         )
+
+    def exp_scores(left_rows, right_rows):
+        scores = lax.dot_general(
+            left_rows, right_rows, (((1,), (1,)), ((), ())), preferred_element_type=F32
+        )
+        return jnp.exp2(scores)
+
+    def quad(q):
+        rows = operand(adv_buf[pl.ds(q * 4, 4), x])
+        total = jnp.zeros((8, BLOCK), F32)
+        for xp in range(4):
+            values = exp_scores(b_ref[xp], rows).reshape(4, 16, 8, BLOCK)
+            for cb in range(4):
+                total = total + jnp.sum(values[cb], axis=0) * wl_buf[xp, pl.ds(q * 4 + cb, 1), :]
+        quarter_buf[z, pl.ds(q, 1), :] = jnp.sum(total, axis=0, keepdims=True)
+
+    for e in (1, 3, 2):
+        arrived(wl_buf.at[at_x(NX - e)], S_WX[e])
+    my_quad = z // 4
+
+    @pl.loop(0, 1)
+    def _(n):
+        quad(my_quad + n)
+
+    for d in (5, -5, 6, -6, 7, -7, 8):
+        pass_on(d)
+
+    @pl.loop(1, 4)
+    def _(n):
+        quad(lax.rem(my_quad + n, 4))
+
+    for d in reversed(ALL_D[1:]):
+        send(quarter_buf.at[z], quarter_buf.at[z], S_QZ[d], to_z(-d))
+
+    for d in ALL_D:
+        for e in (1, 2, 3):
+            arrived(shard(d, NX - e), S_X[d, e])
+
+    @pl.loop(0, 8)
+    def _(p):
+        rows = operand(adv_buf[pl.ds(p * 2, 2)].reshape(8, 16, BLOCK))
         a_ref[p] = rows
         for cb in range(4):
-            scores = lax.dot_general(
-                b_ref[cb * BLOCK : cb * BLOCK + BLOCK, :],
-                rows,
-                (((1,), (1,)), ((), ())),
-                preferred_element_type=F32,
-            )
-            values = jnp.exp2(scores)
-            e_ref[p, cb] = values
-            total = jnp.sum(values, axis=0, keepdims=True)
-            t_ref[cb, pl.ds(p * 2, 1), :] = total[:, 0:128]
-            t_ref[cb, pl.ds(p * 2 + 1, 1), :] = total[:, 128:256]
-
-    def from_x(d):
-        for e in (1, 2, 3):
-            arrived(adv_buf.at[slot(d, NX - e)], S_X[d, e])
-
-    half_z = z // 2
-
-    def chunks(first, count):
-        @pl.loop(0, count)
-        def _(n):
-            far = first + n // 2
-            chunk(lax.rem(half_z + jnp.where(lax.rem(n, 2) == 0, far, 8 - far), 8))
-
-    for d in (0, 1, -1):
-        from_x(d)
-    chunks(0, 1)
-    for d in (2, -2, 3, -3, 4, -4, 5, -5):
-        from_x(d)
-    chunks(1, 4)
-    for d in (6, -6, 7, -7, 8):
-        from_x(d)
-    chunks(3, 3)
-
-    def sum_over_imp(n, part, work):
-        sums[n, 0] = part
-        for e in (2, 1, 3):
-            send(sums.at[n, 0], rx_buf.at[n, e - 1], S_RX[n, e], to_x(e))
-        work(0, 2)
-        for e in (1, 3, 2):
-            arrived(rx_buf.at[n, e - 1], S_RX[n, e])
-        total = part + rx_buf[n, 1] + (rx_buf[n, 0] + rx_buf[n, 2])
-        sums[n, 1] = total
-        index = {d: i for i, d in enumerate(WINDOW + JUMP + (8,))}
-
-        def shift(which, d):
-            send(sums.at[n, which], rz_buf.at[n, index[d]], S_RZ[n, d], to_z(-d))
-
-        for d in (2, -2, 1, -1, 8):
-            shift(1, d)
-        work(2, 4)
-        for d in WINDOW:
-            arrived(rz_buf.at[n, index[d]], S_RZ[n, d])
-        window = total + ((rz_buf[n, 0] + rz_buf[n, 1]) + (rz_buf[n, 2] + rz_buf[n, 3]))
-        sums[n, 2] = window
-        for d in JUMP:
-            shift(2, d)
-        work(4, 8)
-        for d in JUMP + (8,):
-            arrived(rz_buf.at[n, index[d]], S_RZ[n, d])
-        return window + (rz_buf[n, 4] + rz_buf[n, 5]) + rz_buf[n, 6]
+            e_ref[p, cb] = exp_scores(b_ref[x, cb * BLOCK : cb * BLOCK + BLOCK, :], rows)
 
     def tile_values(start, stop):
         @pl.loop(start, stop)
         def _(p):
-            scores = lax.dot_general(
-                a_ref[p], b_ref[...], (((1,), (1,)), ((), ())), preferred_element_type=F32
-            )
-            g_ref[pl.ds(pl.multiple_of(p * 256, 256), 256), :] = jnp.exp2(scores)
+            g_ref[pl.ds(pl.multiple_of(p * 256, 256), 256), :] = exp_scores(a_ref[p], b_ref[x])
+
+    tile_values(0, 3)
+    for d in ALL_D[1:]:
+        arrived(quarter_buf.at[at_z(d)], S_QZ[d])
+    spent = quarter_buf[0]
+    for other in range(1, NZ):
+        spent = spent + quarter_buf[other]
+
+    for k in range(4):
+        turned = pltpu.roll(spent, lax.rem(x - k + 4, 4) * 32, axis=1)
+        turned = jnp.where(place == x, turned, 0.0)
+        for q in range(4):
+            spend_buf[x, 4 * q + k : 4 * q + k + 1, :] = turned[q : q + 1, :]
+    for e in (2, 1, 3):
+        send(spend_buf.at[x], spend_buf.at[x], S_QX[e], to_x(e))
+    tile_values(3, 8)
+    for e in (1, 3, 2):
+        arrived(spend_buf.at[at_x(NX - e)], S_QX[e])
 
     scale = scale_ref[...]
     first_bid = allowance * scale / 32768.0
-    part = t_ref[0] * w_ref[0]
-    for cb in range(1, 4):
-        part = part + t_ref[cb] * w_ref[cb]
-    spending = sum_over_imp(0, part, tile_values) * first_bid
+    spending = ((spend_buf[0] + spend_buf[1]) + (spend_buf[2] + spend_buf[3])) * first_bid
     pacing = allowance / jnp.maximum(spending, allowance)
     row_bid = first_bid * pacing
     for cb in range(4):
@@ -364,7 +408,7 @@
             for cb in range(4):
                 gain = e_ref[p, cb, :, half * 128 : half * 128 + 128] * c2_ref[cb]
                 total = total + jnp.sum(gain.reshape(16, 8, BLOCK), axis=0)
-            t_ref[0, pl.ds(2 * p + half, 1), :] = jnp.sum(total, axis=0, keepdims=True)
+            t_ref[pl.ds(2 * p + half, 1), :] = jnp.sum(total, axis=0, keepdims=True)
 
     def tile_gains(start, stop):
         @pl.loop(start, stop)
@@ -378,13 +422,35 @@
                     bid = value * (first * w_ref[cb, pl.ds(rb, 1), :])
                     g_ref[rows, cb * 128 : cb * 128 + 128] = bid * inverse[cb : cb + 1, :] * value
 
-    spending = sum_over_imp(1, t_ref[0], tile_gains) * scale
+    part = t_ref[...]
+    sums[0] = part
+    for e in (2, 1, 3):
+        send(sums.at[0], rx_buf.at[e - 1], S_RX[e], to_x(e))
+    tile_gains(0, 2)
+    for e in (1, 3, 2):
+        arrived(rx_buf.at[e - 1], S_RX[e])
+    total = part + rx_buf[1] + (rx_buf[0] + rx_buf[2])
+    sums[1] = total
+    index = {d: i for i, d in enumerate(WINDOW + JUMP + (8,))}
+    for d in (2, -2, 1, -1, 8):
+        send(sums.at[1], rz_buf.at[index[d]], S_RZ[d], to_z(-d))
+    tile_gains(2, 4)
+    for d in WINDOW:
+        arrived(rz_buf.at[index[d]], S_RZ[d])
+    window = total + ((rz_buf[0] + rz_buf[1]) + (rz_buf[2] + rz_buf[3]))
+    sums[2] = window
+    for d in JUMP:
+        send(sums.at[2], rz_buf.at[index[d]], S_RZ[d], to_z(-d))
+    tile_gains(4, 8)
+    for copy in started:
+        copy.wait_send()
+    for d in JUMP + (8,):
+        arrived(rz_buf.at[index[d]], S_RZ[d])
+    spending = (window + (rz_buf[4] + rz_buf[5]) + rz_buf[6]) * scale
     pacing = allowance / jnp.maximum(spending, allowance)
     aux_ref[0:16] = scale * pacing * 16384.0
     aux_ref[16:32] = pacing
     aux_ref[32:40] = price
-    for copy in started:
-        copy.wait_send()
 
 
 def scale_kernel(g_ref, aux_ref, out_hbm, price_hbm, pacing_hbm, out_ref, sem):
@@ -427,19 +493,22 @@
             pltpu.VMEM((16, BLOCK), F32),
             pltpu.VMEM((16, BLOCK), jnp.int32),
             pltpu.VMEM((4, 16), jnp.int32),
-            pltpu.VMEM((64, 16, BLOCK), F32),
-            pltpu.VMEM((8, 32, BLOCK), F32),
+            pltpu.VMEM((NZ, NX, 16, BLOCK), F32),
+            pltpu.VMEM((NX, NA, 32, BLOCK), F32),
             pltpu.VMEM((8, 256, 384), BF16),
-            pltpu.VMEM((512, 384), BF16),
+            pltpu.VMEM((NX, 512, 384), BF16),
             pltpu.VMEM((8, 4, BLOCK, 256), F32),
-            pltpu.VMEM((4, 16, BLOCK), F32),
+            pltpu.VMEM((16, BLOCK), F32),
             pltpu.VMEM((NA, 8, BLOCK), F32),
             pltpu.VMEM((NA, 8, BLOCK), F32),
+            pltpu.VMEM((NX, 16, BLOCK), F32),
+            pltpu.VMEM((NZ, 4, BLOCK), F32),
+            pltpu.VMEM((NX, 16, BLOCK), F32),
             pltpu.VMEM((5, 16, BLOCK), F32),
             pltpu.VMEM((4, BLOCK, BLOCK), F32),
-            pltpu.VMEM((2, 3, 16, BLOCK), F32),
-            pltpu.VMEM((2, 3, 16, BLOCK), F32),
-            pltpu.VMEM((2, 7, 16, BLOCK), F32),
+            pltpu.VMEM((3, 16, BLOCK), F32),
+            pltpu.VMEM((3, 16, BLOCK), F32),
+            pltpu.VMEM((7, 16, BLOCK), F32),
             pltpu.VMEM((4, 16, BLOCK), F32),
             pltpu.SemaphoreType.DMA((N_SEM,)),
             pltpu.SemaphoreType.DMA((N_SEM,)),

time: 63.3 us -> 59.3 us (0.937)
  Pallas kernels: 61.7 us -> 58 us
    pallas_call x1, Pallas kernels: 59.5 us -> 55.8 us  [per_device(): pl.pallas_call(exchange_kernel, out_shape=(jax.ShapeDtypeStruct((2048, 51...]
where the time goes in v3:
time: 59.3 us; the launch traced here: 58.7 us
  Pallas kernels  58 us (98%)
  between operations  0.64 us (1%)
    pallas_call x1, Pallas kernels, per_device(): pl.pallas_call(exchange_kernel, out_shape=(jax.ShapeDtypeStruct((2048, 51...  55.8 us
    pallas_call x1, Pallas kernels, per_device(): pl.pallas_call(scale_kernel, out_shape=(jax.ShapeDtypeStruct((2048, 512),...  2.2 us

profile of v3, /device:TPU:6, one launch (start us, length us, event | category | flops | bytes accessed | tf_op | source)
XLA Modules:
  0.0 58.7 jit_solution(12446657770214121011)
XLA Ops:
  0.6 55.8 %exchange.1 = (f32[2048,512]{1,0:T(8,128)S(1)}, f32[40,128]{1,0:T(8,128)S(1)}) custom-call(f32[32,64]{1,0:T(8,128)} %adv_hbm.1, f32[64,64]{1,0:T(8,128)} %imp_hbm.1, f32[16,128]{1,0:T(8,128)} %bitcast.5, s32[16,128]{1,0:T(8,128)} %bitcast.6, s32[4,16]{1,0:T(4,128)} %bitcast.7), custom_call_target="tpu_custom_call" | custom-call | tf_op jit(solution)/shard_map/exchange/pallas_call | solution.py:482
  56.5 2.2 %scale.1 = (f32[2048,512]{1,0:T(8,128)}, f32[4,128]{1,0:T(4,128)}, f32[16,128]{1,0:T(8,128)}) custom-call(f32[2048,512]{1,0:T(8,128)S(1)} %get-tuple-element.8.g_ref, f32[40,128]{1,0:T(8,128)S(1)} %get-tuple-element.9.aux_ref), custom_call_target="tpu_custom_call" | custom-call | tf_op jit(solution)/shard_map/scale/pallas_call | solution.py:533

commit v4 on v3

--- a/solution.py
+++ b/solution.py
@@ -17,6 +17,7 @@
 F32 = jnp.float32
 BF16 = jnp.bfloat16
 
+FAR_Z = (5, -5, 6, -6, 7, -7, 8)
 NEAR = (1, -1, 2, -2, 3, -3, 4, -4)
 FAR_NEG = (1, 2, 3, 4)
 FAR_POS = (1, 2, 3)
@@ -104,6 +105,7 @@
     adv_buf,
     imp_buf,
     a_ref,
+    column_ref,
     b_ref,
     e_ref,
     t_ref,
@@ -266,12 +268,7 @@
             here = imps(e, adv, k)
             arrived(here, S_IY[e, k])
             send(here, here, S_IC[e, k], (partner, imp))
-    for e in range(4):
-        for k in range(4):
-            arrived(imps(e, partner, k), S_IC[e, k])
-
-    @pl.loop(0, 4)
-    def _(xp):
+    def prepare(xp):
         low_half, up_half = twice(imp_buf[xp] * (SCORE_GAIN * LOG2E))
         doubled = jnp.concatenate([low_half, up_half], axis=1).reshape(512, BLOCK)
         high, mid, low = split_parts(doubled)
@@ -300,29 +297,26 @@
         )
         return jnp.exp2(scores)
 
-    def quad(q):
-        rows = operand(adv_buf[pl.ds(q * 4, 4), x])
-        total = jnp.zeros((8, BLOCK), F32)
-        for xp in range(4):
-            values = exp_scores(b_ref[xp], rows).reshape(4, 16, 8, BLOCK)
-            for cb in range(4):
-                total = total + jnp.sum(values[cb], axis=0) * wl_buf[xp, pl.ds(q * 4 + cb, 1), :]
-        quarter_buf[z, pl.ds(q, 1), :] = jnp.sum(total, axis=0, keepdims=True)
-
     for e in (1, 3, 2):
         arrived(wl_buf.at[at_x(NX - e)], S_WX[e])
-    my_quad = z // 4
-
-    @pl.loop(0, 1)
-    def _(n):
-        quad(my_quad + n)
-
-    for d in (5, -5, 6, -6, 7, -7, 8):
+    for e in (0, 1, 3, 2):
+        for k in range(4):
+            arrived(imps(e, partner, k), S_IC[e, k])
+        prepare(at_x(NX - e))
+    for d in FAR_Z:
         pass_on(d)
-
-    @pl.loop(1, 4)
-    def _(n):
-        quad(lax.rem(my_quad + n, 4))
+    column_ref[...] = operand(adv_buf[:, x])
+    totals = [jnp.zeros((8, BLOCK), F32) for _ in range(4)]
+    for e in (0, 1, 3, 2):
+        xp = at_x(NX - e)
+        for cb in range(4):
+            values = exp_scores(b_ref[xp, cb * BLOCK : cb * BLOCK + BLOCK, :], column_ref[...])
+            values = jnp.sum(values.reshape(16, 8, 512), axis=0)
+            for q in range(4):
+                row = wl_buf[xp, 4 * q + cb : 4 * q + cb + 1, :]
+                totals[q] = totals[q] + values[:, q * 128 : q * 128 + 128] * row
+    for q in range(4):
+        quarter_buf[z, q : q + 1, :] = jnp.sum(totals[q], axis=0, keepdims=True)
 
     for d in reversed(ALL_D[1:]):
         send(quarter_buf.at[z], quarter_buf.at[z], S_QZ[d], to_z(-d))
@@ -343,7 +337,6 @@
         def _(p):
             g_ref[pl.ds(pl.multiple_of(p * 256, 256), 256), :] = exp_scores(a_ref[p], b_ref[x])
 
-    tile_values(0, 3)
     for d in ALL_D[1:]:
         arrived(quarter_buf.at[at_z(d)], S_QZ[d])
     spent = quarter_buf[0]
@@ -357,7 +350,6 @@
             spend_buf[x, 4 * q + k : 4 * q + k + 1, :] = turned[q : q + 1, :]
     for e in (2, 1, 3):
         send(spend_buf.at[x], spend_buf.at[x], S_QX[e], to_x(e))
-    tile_values(3, 8)
     for e in (1, 3, 2):
         arrived(spend_buf.at[at_x(NX - e)], S_QX[e])
 
@@ -426,7 +418,7 @@
     sums[0] = part
     for e in (2, 1, 3):
         send(sums.at[0], rx_buf.at[e - 1], S_RX[e], to_x(e))
-    tile_gains(0, 2)
+    tile_values(0, 8)
     for e in (1, 3, 2):
         arrived(rx_buf.at[e - 1], S_RX[e])
     total = part + rx_buf[1] + (rx_buf[0] + rx_buf[2])
@@ -434,7 +426,7 @@
     index = {d: i for i, d in enumerate(WINDOW + JUMP + (8,))}
     for d in (2, -2, 1, -1, 8):
         send(sums.at[1], rz_buf.at[index[d]], S_RZ[d], to_z(-d))
-    tile_gains(2, 4)
+    tile_gains(0, 4)
     for d in WINDOW:
         arrived(rz_buf.at[index[d]], S_RZ[d])
     window = total + ((rz_buf[0] + rz_buf[1]) + (rz_buf[2] + rz_buf[3]))
@@ -496,6 +488,7 @@
             pltpu.VMEM((NZ, NX, 16, BLOCK), F32),
             pltpu.VMEM((NX, NA, 32, BLOCK), F32),
             pltpu.VMEM((8, 256, 384), BF16),
+            pltpu.VMEM((512, 384), BF16),
             pltpu.VMEM((NX, 512, 384), BF16),
             pltpu.VMEM((8, 4, BLOCK, 256), F32),
             pltpu.VMEM((16, BLOCK), F32),

time: 59.3 us -> 58.6 us (0.988)
  no operation moved by 1% of the time
where the time goes in v4:
time: 58.6 us; the launch traced here: 58.4 us
  Pallas kernels  57.8 us (99%)
  between operations  0.64 us (1%)
    pallas_call x1, Pallas kernels, per_device(): pl.pallas_call(exchange_kernel, out_shape=(jax.ShapeDtypeStruct((2048, 51...  55.6 us
    pallas_call x1, Pallas kernels, per_device(): pl.pallas_call(scale_kernel, out_shape=(jax.ShapeDtypeStruct((2048, 512),...  2.2 us

profile of v4, /device:TPU:6, one launch (start us, length us, event | category | flops | bytes accessed | tf_op | source)
XLA Modules:
  0.0 58.4 jit_solution(3389275408025325247)
XLA Ops:
  0.6 55.6 %exchange.1 = (f32[2048,512]{1,0:T(8,128)S(1)}, f32[40,128]{1,0:T(8,128)S(1)}) custom-call(f32[32,64]{1,0:T(8,128)} %adv_hbm.1, f32[64,64]{1,0:T(8,128)} %imp_hbm.1, f32[16,128]{1,0:T(8,128)} %bitcast.5, s32[16,128]{1,0:T(8,128)} %bitcast.6, s32[4,16]{1,0:T(4,128)} %bitcast.7), custom_call_target="tpu_custom_call" | custom-call | tf_op jit(solution)/shard_map/exchange/pallas_call | solution.py:474
  56.2 2.2 %scale.1 = (f32[2048,512]{1,0:T(8,128)}, f32[4,128]{1,0:T(4,128)}, f32[16,128]{1,0:T(8,128)}) custom-call(f32[2048,512]{1,0:T(8,128)S(1)} %get-tuple-element.8.g_ref, f32[40,128]{1,0:T(8,128)S(1)} %get-tuple-element.9.aux_ref), custom_call_target="tpu_custom_call" | custom-call | tf_op jit(solution)/shard_map/scale/pallas_call | solution.py:526

commit v5 on v4

--- a/solution.py
+++ b/solution.py
@@ -309,9 +309,9 @@
     totals = [jnp.zeros((8, BLOCK), F32) for _ in range(4)]
     for e in (0, 1, 3, 2):
         xp = at_x(NX - e)
+        every = exp_scores(b_ref[xp], column_ref[...])
         for cb in range(4):
-            values = exp_scores(b_ref[xp, cb * BLOCK : cb * BLOCK + BLOCK, :], column_ref[...])
-            values = jnp.sum(values.reshape(16, 8, 512), axis=0)
+            values = jnp.sum(every[cb * BLOCK : cb * BLOCK + BLOCK].reshape(16, 8, 512), axis=0)
             for q in range(4):
                 row = wl_buf[xp, 4 * q + cb : 4 * q + cb + 1, :]
                 totals[q] = totals[q] + values[:, q * 128 : q * 128 + 128] * row

time: 58.6 us -> 58 us (0.990)
  Pallas kernels: 57.8 us -> 56.9 us
    pallas_call x1, Pallas kernels: 55.6 us -> 54.7 us  [per_device(): pl.pallas_call(exchange_kernel, out_shape=(jax.ShapeDtypeStruct((2048, 51...]
where the time goes in v5:
time: 58 us; the launch traced here: 57.6 us
  Pallas kernels  56.9 us (98%)
  between operations  0.64 us (1%)
    pallas_call x1, Pallas kernels, per_device(): pl.pallas_call(exchange_kernel, out_shape=(jax.ShapeDtypeStruct((2048, 51...  54.7 us
    pallas_call x1, Pallas kernels, per_device(): pl.pallas_call(scale_kernel, out_shape=(jax.ShapeDtypeStruct((2048, 512),...  2.2 us

profile of v5, /device:TPU:6, one launch (start us, length us, event | category | flops | bytes accessed | tf_op | source)
XLA Modules:
  0.0 57.6 jit_solution(3062049588343275416)
XLA Ops:
  0.6 54.7 %exchange.1 = (f32[2048,512]{1,0:T(8,128)S(1)}, f32[40,128]{1,0:T(8,128)S(1)}) custom-call(f32[32,64]{1,0:T(8,128)} %adv_hbm.1, f32[64,64]{1,0:T(8,128)} %imp_hbm.1, f32[16,128]{1,0:T(8,128)} %bitcast.5, s32[16,128]{1,0:T(8,128)} %bitcast.6, s32[4,16]{1,0:T(4,128)} %bitcast.7), custom_call_target="tpu_custom_call" | custom-call | tf_op jit(solution)/shard_map/exchange/pallas_call | solution.py:474
  55.4 2.2 %scale.1 = (f32[2048,512]{1,0:T(8,128)}, f32[4,128]{1,0:T(4,128)}, f32[16,128]{1,0:T(8,128)}) custom-call(f32[2048,512]{1,0:T(8,128)S(1)} %get-tuple-element.8.g_ref, f32[40,128]{1,0:T(8,128)S(1)} %get-tuple-element.9.aux_ref), custom_call_target="tpu_custom_call" | custom-call | tf_op jit(solution)/shard_map/scale/pallas_call | solution.py:526

commit v6 on v5

--- a/solution.py
+++ b/solution.py
@@ -188,7 +188,7 @@
         load.start()
 
     barrier = pltpu.get_barrier_semaphore()
-    peers = [to_z(d) for d in NEAR] + [to_x(e) for e in (1, 2, 3)] + [to_adv(k) for k in range(1, NA)]
+    peers = [to_z(d) for d in reversed(NEAR)] + [to_x(e) for e in (1, 2, 3)] + [to_adv(k) for k in range(1, NA)]
     for device in peers:
         pl.semaphore_signal(barrier, inc=1, device_id=device, device_id_type=MESH)
 
@@ -197,6 +197,16 @@
     adv_buf[z, x] = jnp.concatenate([adv_in[0:16, :], adv_in[16:32, :]], axis=1)
     loads[1].wait()
     imp_buf[x, adv] = jnp.concatenate([imp_in[0:32, :], imp_in[32:64, :]], axis=1)
+    pl.semaphore_wait(barrier, len(peers))
+
+    for d in (4, -4, 3, -3, 2, -2, 1, -1):
+        send(mine, mine, S_Z[-d], to_z(d))
+    own = imps(0, adv, 0)
+    for e in (2, 1, 3):
+        send(own, own, S_IX[e], to_x(e))
+    for k in (2, 1, 3):
+        send(own, own, S_IY[0, k], to_adv(2 * k))
+    send(own, own, S_IC[0, 0], (partner, imp))
     for load in loads[2:]:
         load.wait()
     allowance = 2.0 * jnp.exp(0.3 * class_ref[...].astype(F32) - 1.2)
@@ -205,17 +215,6 @@
     p1_buf[adv] = jnp.zeros((8, BLOCK), F32)
     for cb in range(4):
         p1_buf[adv, cb : cb + 1, :] = jnp.sum(allowance * mask[:, cb : cb + 1], axis=0, keepdims=True)
-
-    pl.semaphore_wait(barrier, len(peers))
-
-    for d in (4, -4, 3, -3, 2, -2, 1, -1):
-        send(mine, mine, S_Z[-d], to_z(d))
-    own = imps(0, adv, 0)
-    for e in (2, 1, 3):
-        send(own, own, S_IX[e], to_x(e))
-    for k in (2, 1, 3):
-        send(own, own, S_IY[0, k], to_adv(2 * k))
-    send(own, own, S_IC[0, 0], (partner, imp))
     for k in range(1, NA):
         send(p1_buf.at[adv], p1_buf.at[adv], S_P1[k], to_adv(k))
     for e in (2, 1, 3):

time: 58 us -> 58 us (level)
  no operation moved by 1% of the time
where the time goes in v6:
time: 58 us; the launch traced here: 57.5 us
  Pallas kernels  56.9 us (98%)
  between operations  0.64 us (1%)
    pallas_call x1, Pallas kernels, per_device(): pl.pallas_call(exchange_kernel, out_shape=(jax.ShapeDtypeStruct((2048, 51...  54.7 us
    pallas_call x1, Pallas kernels, per_device(): pl.pallas_call(scale_kernel, out_shape=(jax.ShapeDtypeStruct((2048, 512),...  2.2 us

profile of v6, /device:TPU:6, one launch (start us, length us, event | category | flops | bytes accessed | tf_op | source)
XLA Modules:
  0.0 57.5 jit_solution(12404654271173056445)
XLA Ops:
  0.6 54.7 %exchange.1 = (f32[2048,512]{1,0:T(8,128)S(1)}, f32[40,128]{1,0:T(8,128)S(1)}) custom-call(f32[32,64]{1,0:T(8,128)} %adv_hbm.1, f32[64,64]{1,0:T(8,128)} %imp_hbm.1, f32[16,128]{1,0:T(8,128)} %bitcast.5, s32[16,128]{1,0:T(8,128)} %bitcast.6, s32[4,16]{1,0:T(4,128)} %bitcast.7), custom_call_target="tpu_custom_call" | custom-call | tf_op jit(solution)/shard_map/exchange/pallas_call | solution.py:473
  55.3 2.2 %scale.1 = (f32[2048,512]{1,0:T(8,128)}, f32[4,128]{1,0:T(4,128)}, f32[16,128]{1,0:T(8,128)}) custom-call(f32[2048,512]{1,0:T(8,128)S(1)} %get-tuple-element.8.g_ref, f32[40,128]{1,0:T(8,128)S(1)} %get-tuple-element.9.aux_ref), custom_call_target="tpu_custom_call" | custom-call | tf_op jit(solution)/shard_map/scale/pallas_call | solution.py:525
